TPU v7x, 128 devices: a whole 4x4x4 slice. The times are simulated.
128 devices in a mesh: section: 2 (over core), dp: 16 (over y, x), mp: 4 (over z).
Axes of the slice: x: 4, y: 4, z: 4, core: 2. Of those that a mesh axis runs over, the one named last changes fastest.
Arguments:
- patches: bfloat16 [8192, 1280], P(('section', 'dp', 'mp')), may hold values from -6 to 6
- image_units: int32 [128, 3], P(('section', 'dp', 'mp')), may hold values from 1 to 8, 16 in all within a row
- v_gain: float32 [1280], replicated, may hold values from 0.5 to 1.5
- v_qkv: bfloat16 [1280, 3840], replicated, may hold values from -0.15625 to 0.15625
- v_out: bfloat16 [1280, 1280], replicated, may hold values from -0.15625 to 0.15625
- merge_gain: float32 [1280], replicated, may hold values from 0.5 to 1.5
- w_merge: bfloat16 [5120, 8192], P('dp', 'mp'), may hold values from -0.078125 to 0.078125
- routes: int32 [2048, 1], P(('section', 'dp', 'mp')), may hold values from 0 to 15; in each aligned block of 1024 rows (0 to 1023, 1024 to 2047, ...) at most 128 rows name the same one
- text: bfloat16 [4096, 8192], P(('section', 'dp'), 'mp'), may hold values from -6 to 6
- seq_lengths: int32 [32, 3], P(('section', 'dp')), may hold values from 1 to 64, 128 in all within a row
- lang_gain: float32 [2, 8192], P('section'), may hold values from 0.5 to 1.5
- w_qkv: bfloat16 [2, 8192, 5120], P('section', 'dp', 'mp'), may hold values from -0.0625 to 0.0625
- wo_t: bfloat16 [2, 8192, 4096], P('section', 'dp', 'mp'), may hold values from -0.09375 to 0.09375
- row_grads: bfloat16 [4096, 8192], P(('section', 'dp'), 'mp'), may hold values from -6 to 6
Outputs:
- final_hidden: bfloat16 [4096, 8192], P(('section', 'dp'), 'mp')
- merged_grads: bfloat16 [2048, 8192], P(('section', 'dp', 'mp'))
Inputs may be any that keep to these rules, and one draw needn't show every extreme that they name: `image_units`: each row sums to 16. `routes`: among the 1024 rows of one section index (aligned blocks), at most 128 name one group; in some section index one group is named by exactly 128. `seq_lengths`: each row sums to 128.
All inputs are finite; a program needn't handle non-finite values.
Results may differ from a plain program's by a relative error of at most 0.03.
Values may be sent and summed in bfloat16 or wider, within the bound.
A program may use at most 192 MiB of HBM per device.

v0:
```python
import math
import jax
import jax.numpy as jnp
from jax import lax
from jax.sharding import PartitionSpec as P

QH = 32
KVH = 4
HD = 128
VD = 1280
VH = 16
VHD = 80
MERGE = 4
EPSILON = 1e-06


def passed_along(value, axis, steps):
    count = lax.axis_size(axis)
    initial, last = (max(0, -steps), min(count, count - steps))
    return lax.ppermute(value, axis, [(source, source + steps) for source in range(initial, last)])


def broadcast(block, axis, owner):
    block = jnp.where(lax.axis_index(axis) == owner, block, jnp.zeros_like(block))
    return lax.psum(block, axis)


def layer_norm(values, norm_gain):
    values = values.astype(jnp.float32)
    centre = jnp.mean(values, axis=-1, keepdims=True)
    centred = values - centre
    variance = jnp.mean(centred * centred, axis=-1, keepdims=True)
    return centred * lax.rsqrt(variance + EPSILON) * norm_gain


def rms_norm(values, norm_gain):
    values = values.astype(jnp.float32)
    return (
        values * lax.rsqrt(jnp.mean(values * values, axis=-1, keepdims=True) + EPSILON) * norm_gain
    )


def segment_of(lengths, amount):
    boundary = jnp.cumsum(lengths.astype(jnp.int32))
    positions = jnp.arange(amount, dtype=jnp.int32)
    return jnp.sum((positions[:, None] >= boundary[None, :]).astype(jnp.int32), axis=1)


def vision_rows(patches, units, v_gain, v_qkv, v_out, merge_gain):
    amount = patches.shape[0]
    merged_count = amount // MERGE
    unit_image = segment_of(units, merged_count)
    image_ids = jnp.broadcast_to(unit_image[:, None], (merged_count, MERGE)).reshape(amount)
    v_normed = layer_norm(patches, v_gain).astype(jnp.bfloat16)
    projected = jnp.dot(v_normed, v_qkv, preferred_element_type=jnp.float32).astype(jnp.bfloat16)
    projected = projected.reshape(amount, 3, VH, VHD)
    scores = jnp.einsum(
        "qhd,khd->hqk", projected[:, 0], projected[:, 1], preferred_element_type=jnp.float32
    ) / math.sqrt(VHD)
    allowed = image_ids[:, None] == image_ids[None, :]
    scores = jnp.where(allowed[None], scores, -1e30)
    weights = jax.nn.softmax(scores, axis=-1).astype(jnp.bfloat16)
    attended = (
        jnp.einsum("hqk,khd->qhd", weights, projected[:, 2], preferred_element_type=jnp.float32)
        .astype(jnp.bfloat16)
        .reshape(amount, VD)
    )
    update = jnp.dot(attended, v_out, preferred_element_type=jnp.float32)
    v_hidden = (patches.astype(jnp.float32) + update).astype(jnp.bfloat16)
    merged = layer_norm(v_hidden, merge_gain).astype(jnp.bfloat16)
    return merged.reshape(merged_count, MERGE * VD)


def attend(projected, lengths):
    seq_rows = projected.shape[0]
    group_size = QH // KVH
    kv_here = projected.shape[1] // ((group_size + 2) * HD)
    heads_view = projected.reshape(seq_rows, kv_here, group_size + 2, HD)
    scores = jnp.einsum(
        "tkgd,skd->kgts",
        heads_view[:, :, :group_size],
        heads_view[:, :, group_size],
        preferred_element_type=jnp.float32,
    ) * (1.0 / math.sqrt(HD))
    seq_ids = segment_of(lengths, seq_rows)
    positions = jnp.arange(seq_rows, dtype=jnp.int32)
    allowed = (seq_ids[:, None] == seq_ids[None, :]) & (positions[:, None] >= positions[None, :])
    scores = jnp.where(allowed[None, None], scores, -1e30)
    weights = jax.nn.softmax(scores, axis=-1).astype(jnp.bfloat16)
    attended = jnp.einsum(
        "kgts,skd->tkgd",
        weights,
        heads_view[:, :, group_size + 1],
        preferred_element_type=jnp.float32,
    ).astype(jnp.bfloat16)
    return attended.reshape(seq_rows, kv_here * group_size * HD)


def shards(
    patches,
    image_units,
    v_gain,
    v_qkv,
    v_out,
    merge_gain,
    w_merge,
    routes,
    text,
    seq_lengths,
    lang_gain,
    w_qkv,
    wo_t,
    row_grads,
):
    merged = vision_rows(patches, image_units[0], v_gain, v_qkv, v_out, merge_gain)
    all_rows, all_routes = (
        lax.all_gather(merged, ("dp", "mp"), axis=0, tiled=True),
        lax.all_gather(routes, ("dp", "mp"), axis=0, tiled=True),
    )
    target = all_routes[:, 0]
    section_rows = target.shape[0]
    row_order = jnp.arange(section_rows, dtype=jnp.int32)
    matching = target[:, None] == target[None, :]
    position = jnp.sum(
        (matching & (row_order[:, None] > row_order[None, :])).astype(jnp.int32), axis=1
    )
    seq_rows = text.shape[0]
    slot_index = target * seq_rows + position
    group_here = lax.axis_index("dp")
    dp_count = lax.axis_size("dp")
    slice_width = w_merge.shape[0]
    row_slice = lax.dynamic_slice_in_dim(all_rows, group_here * slice_width, slice_width, 1)
    wanted = jnp.arange(seq_rows * lax.axis_size("dp"), dtype=jnp.int32)
    picker = (slot_index[None, :] == wanted[:, None]).astype(jnp.bfloat16)
    picked = jnp.dot(picker, row_slice, preferred_element_type=jnp.float32).astype(jnp.bfloat16)
    image_rows = lax.psum_scatter(
        jnp.dot(picked, w_merge, preferred_element_type=jnp.float32).astype(jnp.bfloat16),
        "dp",
        scatter_dimension=0,
        tiled=True,
    )
    present = jnp.sum((target == group_here).astype(jnp.int32))
    positions = jnp.arange(seq_rows, dtype=jnp.int32)
    entry_rows = jnp.where((positions < present)[:, None], image_rows, text)
    gathered = (
        lax.all_gather(w_qkv, "dp", axis=1, tiled=True),
        lax.all_gather(wo_t, "dp", axis=1, tiled=True),
    )
    qkv_weight = gathered[0][0]
    out_weight = gathered[1][0]
    norm_gain = lang_gain[0]
    sections = lax.axis_size("section")
    section_here = lax.axis_index("section")
    is_first = section_here == 0
    lengths_here = seq_lengths[0]
    entry_all, lengths_all = (
        lax.all_gather(entry_rows, "section", axis=0, tiled=True),
        lax.all_gather(seq_lengths, "section", axis=0, tiled=True),
    )
    carried = jnp.zeros_like(entry_rows)
    carried_lengths = lengths_here
    finished = []
    for section_step in range(2 * sections - 1):
        if section_step > 0:
            carried, carried_lengths = passed_along((carried, carried_lengths), "section", 1)
        if section_step < sections:
            incoming = entry_all[section_step * seq_rows : (section_step + 1) * seq_rows]
            incoming_lengths = lengths_all[section_step]
            carried = jnp.where(is_first, incoming, carried)
            carried_lengths = jnp.where(is_first, incoming_lengths, carried_lengths)
        features = lax.all_gather(carried, "mp", axis=1, tiled=True)
        normed = rms_norm(features, norm_gain).astype(jnp.bfloat16)
        projected = jnp.dot(normed, qkv_weight, preferred_element_type=jnp.float32)
        attended = attend(projected.astype(jnp.bfloat16), carried_lengths)
        partial_value = lax.dot_general(
            attended, out_weight, (((1,), (1,)), ((), ())), preferred_element_type=jnp.float32
        )
        update = lax.psum_scatter(
            partial_value.astype(jnp.bfloat16), "mp", scatter_dimension=1, tiled=True
        ).astype(jnp.float32)
        carried = (carried.astype(jnp.float32) + update).astype(jnp.bfloat16)
        if section_step >= sections - 1:
            finished.append(carried)
    returned_rows = broadcast(jnp.stack(finished), "section", sections - 1)
    final_hidden = lax.dynamic_index_in_dim(returned_rows, section_here, 0, keepdims=False)
    columns = row_grads.shape[1]
    picker = ((target == group_here)[:, None] & (position[:, None] == positions[None, :])).astype(
        jnp.bfloat16
    )
    outgoing = jnp.dot(picker, row_grads, preferred_element_type=jnp.float32).astype(jnp.bfloat16)
    outgoing = outgoing.reshape(dp_count, section_rows // dp_count, columns)
    returned = lax.all_to_all(
        lax.all_to_all(outgoing, "dp", split_axis=0, concat_axis=0, tiled=True),
        "mp",
        split_axis=1,
        concat_axis=2,
        tiled=True,
    )
    merged_grads = jnp.sum(returned.astype(jnp.float32), axis=0).astype(jnp.bfloat16)
    return (final_hidden, merged_grads)


def solution(mesh):
    in_specs = (
        P(("section", "dp", "mp"), None),
        P(("section", "dp", "mp"), None),
        P(),
        P(),
        P(),
        P(),
        P("dp", "mp"),
        P(("section", "dp", "mp"), None),
        P(("section", "dp"), "mp"),
        P(("section", "dp"), None),
        P("section", None),
        P("section", "dp", "mp"),
        P("section", "dp", "mp"),
        P(("section", "dp"), "mp"),
    )
    out_specs = (P(("section", "dp"), "mp"), P(("section", "dp", "mp"), None))
    return jax.shard_map(shards, mesh=mesh, in_specs=in_specs, out_specs=out_specs, check_vma=False)
```

profile of v0, /device:TPU:0, one launch (start us, length us, event | category | flops | bytes accessed | tf_op | source)
XLA Modules:
  0.0 799.6 jit_solution(8067572202809848577)
XLA Ops:
  9.6 6.6 convolution_convert_fusion.1
  34.4 24.9 %all-reduce = s32[1024]{0:T(1024)S(1)} all-reduce(s32[1024]{0:T(1024)S(1)} %bitcast_dynamic-update-slice_fusion), channel_id=1, replica_groups=mesh['section'=2,'dp'=16,'mp'=4] {'dp','mp'}, use_global_device_ids=true, to_apply=%add | all-reduce | flops 1024 | bytes 8192 | tf_op jit(solution)/shard_map/squeeze | solution.py:120
  60.4 60.5 %all-gather.9.cloned.1.call-done = bf16[1024,5120]{1,0:T(8,128)(2,1)} async-done(((bf16[16,5120]{1,0:T(8,128)(2,1)}), bf16[1024,5120]{1,0:T(8,128)(2,1)}) %all-gather.9.cloned.1.call-update) | async-done | bytes 10485776 | tf_op jit(solution)/shard_map/all_gather | solution.py:117
  120.9 10.7 %convolution_convert_fusion = bf16[2048,2048]{1,0:T(8,128)(2,1)} fusion(bf16[320,2048]{1,0:T(8,128)(2,1)} %param.20, s32[1024]{0:T(1024)S(1)} %get-tuple-element.7, bf16[1024,5120]{1,0:T(8,128)(2,1)} %all-gather.9.cloned.1.call-done, s32[]{:T(128)S(6)} %select_n.69), kind=kOutput, calls=%fused_computation.18 | convolution fusion | flops 4033478656 | bytes 10489860 | tf_op jit(solution)/shard_map/dot_general | solution.py:137
  132.4 83.8 %reduce-scatter.5.cloned.1.call-done = bf16[128,2048]{1,0:T(8,128)(2,1)} async-done(((bf16[2048,2048]{1,0:T(8,128)(2,1)}), bf16[128,2048]{1,0:T(8,128)(2,1)}) %reduce-scatter.5.cloned.1.call-update) | async-done | bytes 524304 | tf_op jit(solution)/shard_map/reduce_scatter | solution.py:136
  218.3 11.4 %all-gather.11.cloned.1.call-done = bf16[256,2048]{1,0:T(8,128)(2,1)} async-done(((bf16[128,2048]{1,0:T(8,128)(2,1)}), bf16[256,2048]{1,0:T(8,128)(2,1)}) %all-gather.11.cloned.1.call-update) | async-done | bytes 1048592 | tf_op jit(solution)/shard_map/all_gather | solution.py:157
  235.4 28.8 %all-gather.13.cloned.1.call-done = bf16[128,8192]{1,0:T(8,128)(2,1)} async-done(((bf16[128,2048]{1,0:T(8,128)(2,1)}), bf16[128,8192]{1,0:T(8,128)(2,1)}) %all-gather.13.cloned.1.call-update) | async-done | bytes 2097168 | tf_op jit(solution)/shard_map/all_gather | solution.py:171
  266.3 132.4 %all-gather.15.cloned.1.call-done = bf16[1,8192,1280]{2,1,0:T(8,128)(2,1)} async-done(((bf16[1,512,1280]{2,1,0:T(8,128)(2,1)}), bf16[1,8192,1280]{2,1,0:T(8,128)(2,1)}) %all-gather.15.cloned.1.call-update) | async-done | bytes 20971536 | tf_op jit(solution)/shard_map/all_gather | solution.py:146
  398.7 10.6 %fusion.35 = bf16[128,1280]{1,0:T(8,128)(2,1)S(1)} fusion(bf16[1,8192,1280]{2,1,0:T(8,128)(2,1)} %all-gather.15.cloned.1.call-done, bf16[128,8192]{1,0:T(8,128)(2,1)} %all-gather.13.cloned.1.call-done, f32[8192]{0:T(1024)S(1)} %bitcast.203, f32[128]{0:T(128)S(1)} %add_rsqrt_fusion.2), kind=kOutput, calls=%fused_computation.41 | convolution fusion | flops 2688712704 | bytes 23429632 | tf_op jit(solution)/shard_map/dot_general | solution.py:173
  410.1 101.6 %all-gather.17.cloned.1.call-done = bf16[1,8192,1024]{2,1,0:T(8,128)(2,1)} async-done(((bf16[1,512,1024]{2,1,0:T(8,128)(2,1)}), bf16[1,8192,1024]{2,1,0:T(8,128)(2,1)}) %all-gather.17.cloned.1.call-update) | async-done | bytes 16777232 | tf_op jit(solution)/shard_map/all_gather | solution.py:147
  511.7 12.8 %fusion.13 = bf16[128,8192]{1,0:T(8,128)(2,1)} fusion(bf16[128,1024]{0,1:T(8,128)(2,1)S(1)} %bitcast.197, bf16[1,8192,1024]{2,1,0:T(8,128)(2,1)} %all-gather.17.cloned.1.call-done), kind=kOutput, calls=%fused_computation.13 | convolution fusion | flops 2148532224 | bytes 19136512 | tf_op jit(solution)/shard_map/dot_general | solution.py:175
  524.6 29.7 %reduce-scatter.7.cloned.1.call-done = bf16[128,2048]{1,0:T(8,128)(2,1)} async-done(((bf16[128,8192]{1,0:T(8,128)(2,1)}), bf16[128,2048]{1,0:T(8,128)(2,1)}) %reduce-scatter.7.cloned.1.call-update) | async-done | bytes 524304 | tf_op jit(solution)/shard_map/reduce_scatter | solution.py:178
  563.2 27.3 %all-gather.19.cloned.1.call-done = bf16[128,8192]{1,0:T(8,128)(2,1)} async-done(((bf16[128,2048]{1,0:T(8,128)(2,1)}), bf16[128,8192]{1,0:T(8,128)(2,1)}) %all-gather.19.cloned.1.call-update) | async-done | bytes 2097168 | tf_op jit(solution)/shard_map/all_gather | solution.py:171
  592.6 10.6 %fusion.38 = bf16[128,1280]{1,0:T(8,128)(2,1)S(1)} fusion(bf16[1,8192,1280]{2,1,0:T(8,128)(2,1)} %all-gather.15.cloned.1.call-done, bf16[128,8192]{1,0:T(8,128)(2,1)} %all-gather.19.cloned.1.call-done, f32[128]{0:T(128)S(1)} %add_rsqrt_fusion.1, f32[8192]{0:T(1024)S(1)} %bitcast.204), kind=kOutput, calls=%fused_computation.42 | convolution fusion | flops 2688712704 | bytes 23429632 | tf_op jit(solution)/shard_map/dot_general | solution.py:173
  604.0 12.8 %fusion.16 = bf16[128,8192]{1,0:T(8,128)(2,1)} fusion(bf16[128,1024]{0,1:T(8,128)(2,1)S(1)} %bitcast.199, bf16[1,8192,1024]{2,1,0:T(8,128)(2,1)} %all-gather.17.cloned.1.call-done), kind=kOutput, calls=%fused_computation.14 | convolution fusion | flops 2148532224 | bytes 19136512 | tf_op jit(solution)/shard_map/dot_general | solution.py:175
  616.9 29.9 %reduce-scatter.9.cloned.1.call-done = bf16[128,2048]{1,0:T(8,128)(2,1)} async-done(((bf16[128,8192]{1,0:T(8,128)(2,1)}), bf16[128,2048]{1,0:T(8,128)(2,1)}) %reduce-scatter.9.cloned.1.call-update) | async-done | bytes 524304 | tf_op jit(solution)/shard_map/reduce_scatter | solution.py:178
  655.2 6.9 all-to-all-start
  665.3 17.6 %all-gather.21.cloned.1.call-done = bf16[128,8192]{1,0:T(8,128)(2,1)} async-done(((bf16[128,2048]{1,0:T(8,128)(2,1)}), bf16[128,8192]{1,0:T(8,128)(2,1)}) %all-gather.21.cloned.1.call-update) | async-done | bytes 2097168 | tf_op jit(solution)/shard_map/all_gather | solution.py:171
  685.0 10.6 %fusion.41 = bf16[128,1280]{1,0:T(8,128)(2,1)S(1)} fusion(bf16[1,8192,1280]{2,1,0:T(8,128)(2,1)} %all-gather.15.cloned.1.call-done, bf16[128,8192]{1,0:T(8,128)(2,1)} %all-gather.21.cloned.1.call-done, f32[128]{0:T(128)S(1)} %add_rsqrt_fusion, f32[8192]{0:T(1024)S(1)} %bitcast.205), kind=kOutput, calls=%fused_computation.43 | convolution fusion | flops 2688712704 | bytes 23429632 | tf_op jit(solution)/shard_map/dot_general | solution.py:173
  696.5 12.8 %fusion.19 = bf16[128,8192]{1,0:T(8,128)(2,1)} fusion(bf16[128,1024]{0,1:T(8,128)(2,1)S(1)} %bitcast.198, bf16[1,8192,1024]{2,1,0:T(8,128)(2,1)} %all-gather.17.cloned.1.call-done), kind=kOutput, calls=%fused_computation.15 | convolution fusion | flops 2148532224 | bytes 19136512 | tf_op jit(solution)/shard_map/dot_general | solution.py:175
  709.3 16.7 %all-to-all-done = bf16[16,64,2048]{2,1,0:T(8,128)(2,1)} async-done(((bf16[16,64,2048]{2,1,0:T(8,128)(2,1)}), bf16[16,64,2048]{2,1,0:T(8,128)(2,1)}, u32[]{:S(2)}, u32[]{:S(2)}) %all-to-all-start) | async-done | bytes 4194336 | tf_op jit(solution)/shard_map/all_to_all | solution.py:193
  726.0 6.5 copy.122
  732.5 5.0 all-to-all-start.1
  742.8 43.2 %all-to-all-done.1 = bf16[16,64,2048]{2,0,1:T(8,128)(2,1)} async-done(((bf16[16,64,2048]{2,0,1:T(8,128)(2,1)}), bf16[16,64,2048]{2,0,1:T(8,128)(2,1)}, u32[]{:S(2)}, u32[]{:S(2)}) %all-to-all-start.1) | async-done | bytes 4194336 | tf_op jit(solution)/shard_map/all_to_all | solution.py:192
  (137 shorter events, 70.5 us)
Async XLA Ops:
  7.2 113.7 %all-gather.9.cloned.1.call-start = ((), (), s32[]{:S(2)}) async-start(), calls=%async_computation.6 | async-start | bytes 10649600 | tf_op jit(solution)/shard_map/all_gather | solution.py:117
  32.9 183.3 %reduce-scatter.5.cloned.1.call-start = ((), (), s32[]{:S(2)}) async-start(), calls=%async_computation.7 | async-start | bytes 8912896 | tf_op jit(solution)/shard_map/reduce_scatter | solution.py:136
  131.6 84.6 %copy-start.9 = (bf16[128,2048]{1,0:T(8,128)(2,1)S(1)}, bf16[128,2048]{1,0:T(8,128)(2,1)}, u32[]{:S(2)}) copy-start(bf16[128,2048]{1,0:T(8,128)(2,1)} %param.22) | copy-start | bytes 1572868
  131.7 101.1 %copy-start.11 = (s32[1,3]{1,0:T(1,128)S(1)}, s32[1,3]{1,0:T(1,128)}, u32[]{:S(2)}) copy-start(s32[1,3]{1,0:T(1,128)} %param.23) | copy-start | bytes 40
  131.7 267.0 %copy-start.12 = (f32[1,8192]{1,0:T(1,128)S(1)}, f32[1,8192]{1,0:T(1,128)}, u32[]{:S(2)}) copy-start(f32[1,8192]{1,0:T(1,128)} %param.24) | copy-start | bytes 98308
  131.7 98.0 %all-gather.11.cloned.1.call-start = ((), (), s32[]{:S(2)}) async-start(), calls=%async_computation.8 | async-start | bytes 1572864 | tf_op jit(solution)/shard_map/all_gather | solution.py:157
  218.2 46.0 %all-gather.13.cloned.1.call-start = ((), (), s32[]{:S(2)}) async-start(), calls=%async_computation.9 | async-start | bytes 2621440 | tf_op jit(solution)/shard_map/all_gather | solution.py:171
  231.6 167.1 %all-gather.15.cloned.1.call-start = ((), (), s32[]{:S(2)}) async-start(), calls=%async_computation.10 | async-start | bytes 22282240 | tf_op jit(solution)/shard_map/all_gather | solution.py:146
  232.2 279.5 %all-gather.17.cloned.1.call-start = ((), (), s32[]{:S(2)}) async-start(), calls=%async_computation.11 | async-start | bytes 17825792 | tf_op jit(solution)/shard_map/all_gather | solution.py:147
  232.7 321.6 %reduce-scatter.7.cloned.1.call-start = ((), (), s32[]{:S(2)}) async-start(), calls=%async_computation.12 | async-start | bytes 2621440 | tf_op jit(solution)/shard_map/reduce_scatter | solution.py:178
  511.7 42.6 %copy-start.4 = (bf16[256,2048]{1,0:T(8,128)(2,1)S(1)}, bf16[256,2048]{1,0:T(8,128)(2,1)}, u32[]{:S(2)}) copy-start(bf16[256,2048]{1,0:T(8,128)(2,1)} %all-gather.11.cloned.1.call-done) | copy-start | bytes 3145732
  524.5 66.0 %all-gather.19.cloned.1.call-start = ((), (), s32[]{:S(2)}) async-start(), calls=%async_computation.13 | async-start | bytes 2621440 | tf_op jit(solution)/shard_map/all_gather | solution.py:171
  555.5 3.3 collective-permute-start
  559.7 87.1 %reduce-scatter.9.cloned.1.call-start = ((), (), s32[]{:S(2)}) async-start(), calls=%async_computation.14 | async-start | bytes 2621440 | tf_op jit(solution)/shard_map/reduce_scatter | solution.py:178
  559.8 3.1 collective-permute-start.1
  604.0 42.7 %copy-start.2 = (bf16[128,2048]{1,0:T(8,128)(2,1)S(1)}, bf16[128,2048]{1,0:T(8,128)(2,1)}, u32[]{:S(2)}) copy-start(bf16[128,2048]{1,0:T(8,128)(2,1)} %slice_select_fusion.1) | copy-start | bytes 1572868
  616.9 66.1 %all-gather.21.cloned.1.call-start = ((), (), s32[]{:S(2)}) async-start(), calls=%async_computation.15 | async-start | bytes 2621440 | tf_op jit(solution)/shard_map/all_gather | solution.py:171
  648.0 3.3 collective-permute-start.2
  655.2 70.8 %all-to-all-start = ((bf16[16,64,2048]{2,1,0:T(8,128)(2,1)}), bf16[16,64,2048]{2,1,0:T(8,128)(2,1)}, u32[]{:S(2)}, u32[]{:S(2)}) async-start(bf16[16,64,2048]{2,1,0:T(8,128)(2,1)} %bitcast.188), calls=%async_computation.4 | async-start | bytes 8388608 | tf_op jit(solution)/shard_map/all_to_all | solution.py:193
  662.1 77.1 %reduce-scatter.11.cloned.1.call-start = ((), (), s32[]{:S(2)}) async-start(), calls=%async_computation.16 | async-start | bytes 2621440 | tf_op jit(solution)/shard_map/reduce_scatter | solution.py:178
  662.1 2.8 collective-permute-start.3
  732.5 53.5 %all-to-all-start.1 = ((bf16[16,64,2048]{2,0,1:T(8,128)(2,1)}), bf16[16,64,2048]{2,0,1:T(8,128)(2,1)}, u32[]{:S(2)}, u32[]{:S(2)}) async-start(bf16[16,64,2048]{2,0,1:T(8,128)(2,1)} %copy.122), calls=%async_computation.5 | async-start | bytes 8388608 | tf_op jit(solution)/shard_map/all_to_all | solution.py:192
  737.5 53.2 %all-reduce.3.cloned.1.call-start = ((), (), s32[]{:S(2)}) async-start(), calls=%async_computation.17 | async-start | bytes 2097152 | tf_op jit(solution)/shard_map/psum | solution.py:25
  740.4 52.1 %copy-start.1 = (bf16[1280,1280]{1,0:T(8,128)(2,1)S(1)}, bf16[1280,1280]{1,0:T(8,128)(2,1)}, u32[]{:S(2)}) copy-start(bf16[1280,1280]{1,0:T(8,128)(2,1)} %param.18) | copy-start | bytes 9830404
  (11 other events, 127.5 us)
Sparse Core Ops, SparseCore 0:
  33.0 87.8 all-gather.8
  131.8 84.4 reduce-scatter.4
  218.5 11.1 all-gather.10
  231.8 32.4 all-gather.12
  266.2 132.4 all-gather.14
  400.7 110.9 all-gather.16
  524.7 29.5 reduce-scatter.6
  559.8 30.6 all-gather.18
  617.0 29.7 reduce-scatter.8
  652.2 30.6 all-gather.20
  709.4 29.7 reduce-scatter.10
  742.9 26.6 all-reduce.2
where the time goes:
time: 808 us; the launch traced here: 800 us
  waiting for transfers between devices  590 us (73%)
  matrix products  97.5 us (12%)
  blocking collectives  27.2 us (3%)
  other arithmetic  27.1 us (3%)
  local copies, waits for them, and re-layouts  21.7 us (3%)
  starting transfers between devices  20.7 us (3%)
  between operations  15.5 us (2%)
    all_gather x1, waiting for transfers between devices, shards(): lax.all_gather(w_qkv, 'dp', axis=1, tiled=True)  132 us
    all_gather x1, waiting for transfers between devices, shards(): lax.all_gather(wo_t, 'dp', axis=1, tiled=True)  102 us
    reduce_scatter x1, waiting for transfers between devices, shards(): lax.psum_scatter(jnp.dot(picked, w_merge, preferred_element_type=jnp.floa...  83.8 us
    all_gather x3, waiting for transfers between devices, shards(): features = lax.all_gather(carried, 'mp', axis=1, tiled=True)  73.8 us
    reduce_scatter x3, waiting for transfers between devices, shards(): lax.psum_scatter(partial_value.astype(jnp.bfloat16), 'mp', scatter_dimens...  61.3 us
    all_gather x1, waiting for transfers between devices, shards(): lax.all_gather(merged, ('dp', 'mp'), axis=0, tiled=True)  60.5 us
    all_to_all x1, waiting for transfers between devices, shards(): lax.all_to_all(lax.all_to_all(outgoing, 'dp', split_axis=0, concat_axis=0...  43.2 us
    dot_general x3, matrix products, shards(): lax.dot_general(attended, out_weight, (((1,), (1,)), ((), ())), preferred...  38.4 us
  transfers between devices with their start and end apart: 18, of which 17 were waited for; matrix products, arithmetic and copies ran while one was open for 8% of the time, Pallas kernels for 0%

commit v1 on v0

--- a/solution.py
+++ b/solution.py
@@ -168,7 +168,26 @@
             incoming_lengths = lengths_all[section_step]
             carried = jnp.where(is_first, incoming, carried)
             carried_lengths = jnp.where(is_first, incoming_lengths, carried_lengths)
-        features = lax.all_gather(carried, "mp", axis=1, tiled=True)
+        length, mine, rows = (lax.axis_size("mp"), lax.axis_index("mp"), carried.shape[1])
+        right = [(i, (i + 1) % length) for i in range(length)]
+        left = [(i, (i - 1) % length) for i in range(length)]
+        result = jnp.zeros(
+            (*carried.shape[:1], length * rows, *carried.shape[1 + 1 :]), carried.dtype
+        )
+        result = lax.dynamic_update_slice_in_dim(result, carried, mine * rows, axis=1)
+        from_left = from_right = carried
+        middle = length // 2
+        for turn in range(1, middle + 1):
+            from_left = lax.ppermute(from_left, "mp", right)
+            result = lax.dynamic_update_slice_in_dim(
+                result, from_left, (mine - turn) % length * rows, axis=1
+            )
+            if turn < length - middle:
+                from_right = lax.ppermute(from_right, "mp", left)
+                result = lax.dynamic_update_slice_in_dim(
+                    result, from_right, (mine + turn) % length * rows, axis=1
+                )
+        features = result
         normed = rms_norm(features, norm_gain).astype(jnp.bfloat16)
         projected = jnp.dot(normed, qkv_weight, preferred_element_type=jnp.float32)
         attended = attend(projected.astype(jnp.bfloat16), carried_lengths)

time: 808 us -> 771 us (0.954)
  waiting for transfers between devices: 590 us -> 548 us
  starting transfers between devices: 20.7 us -> 31.1 us
    all_gather x3 -> x0, waiting for transfers between devices: 73.8 us -> none  [shards(): features = lax.all_gather(carried, 'mp', axis=1, tiled=True)]
    ppermute x0 -> x9, waiting for transfers between devices: none -> 59.3 us  [the longest x6 45.5 us: shards(): from_left = lax.ppermute(from_left, 'mp', right)]
    all_gather x1, waiting for transfers between devices: 132 us -> 102 us  [shards(): lax.all_gather(w_qkv, 'dp', axis=1, tiled=True)]
    ppermute x0 -> x9, starting transfers between devices: none -> 10.9 us  [the longest x3 7.65 us: shards(): from_right = lax.ppermute(from_right, 'mp', left)]
  transfers between devices with their start and end apart: 18 -> 24, of which waited for: 17 -> 22; matrix products, arithmetic and copies ran while one was open for 8% -> 8% of each run, Pallas kernels for 0% -> 0%
where the time goes in v1:
time: 771 us; the launch traced here: 762 us
  waiting for transfers between devices  548 us (71%)
  matrix products  95.4 us (12%)
  starting transfers between devices  31.1 us (4%)
  blocking collectives  26.7 us (3%)
  local copies, waits for them, and re-layouts  25.1 us (3%)
  other arithmetic  20.6 us (3%)
  between operations  15.3 us (2%)
    all_gather x1, waiting for transfers between devices, shards(): lax.all_gather(w_qkv, 'dp', axis=1, tiled=True)  102 us
    all_gather x1, waiting for transfers between devices, shards(): lax.all_gather(wo_t, 'dp', axis=1, tiled=True)  102 us
    reduce_scatter x1, waiting for transfers between devices, shards(): lax.psum_scatter(jnp.dot(picked, w_merge, preferred_element_type=jnp.floa...  84 us
    all_gather x1, waiting for transfers between devices, shards(): lax.all_gather(merged, ('dp', 'mp'), axis=0, tiled=True)  60.5 us
    reduce_scatter x3, waiting for transfers between devices, shards(): lax.psum_scatter(partial_value.astype(jnp.bfloat16), 'mp', scatter_dimens...  58.5 us
    all_to_all x1, waiting for transfers between devices, shards(): lax.all_to_all(lax.all_to_all(outgoing, 'dp', split_axis=0, concat_axis=0...  46.1 us
    ppermute x6, waiting for transfers between devices, shards(): from_left = lax.ppermute(from_left, 'mp', right)  45.5 us
    dot_general x3, matrix products, shards(): lax.dot_general(attended, out_weight, (((1,), (1,)), ((), ())), preferred...  38.3 us
  transfers between devices with their start and end apart: 24, of which 22 were waited for; matrix products, arithmetic and copies ran while one was open for 8% of the time, Pallas kernels for 0%

profile of v1, /device:TPU:0, one launch (start us, length us, event | category | flops | bytes accessed | tf_op | source)
XLA Modules:
  0.0 761.8 jit_solution(9126136771049095027)
XLA Ops:
  9.6 6.6 convolution_convert_fusion.1
  34.4 24.9 %all-reduce = s32[1024]{0:T(1024)S(1)} all-reduce(s32[1024]{0:T(1024)S(1)} %bitcast_dynamic-update-slice_fusion), channel_id=1, replica_groups=mesh['section'=2,'dp'=16,'mp'=4] {'dp','mp'}, use_global_device_ids=true, to_apply=%add | all-reduce | flops 1024 | bytes 8192 | tf_op jit(solution)/shard_map/squeeze | solution.py:120
  60.5 60.5 %all-gather.6.cloned.1.call-done = bf16[1024,5120]{1,0:T(8,128)(2,1)} async-done(((bf16[16,5120]{1,0:T(8,128)(2,1)}), bf16[1024,5120]{1,0:T(8,128)(2,1)}) %all-gather.6.cloned.1.call-update) | async-done | bytes 10485776 | tf_op jit(solution)/shard_map/all_gather | solution.py:117
  120.9 10.7 %convolution_convert_fusion = bf16[2048,2048]{1,0:T(8,128)(2,1)} fusion(bf16[320,2048]{1,0:T(8,128)(2,1)} %param.20, s32[1024]{0:T(1024)S(1)} %get-tuple-element.11, bf16[1024,5120]{1,0:T(8,128)(2,1)} %all-gather.6.cloned.1.call-done, s32[]{:T(128)S(6)} %select_n.116), kind=kOutput, calls=%fused_computation.18 | convolution fusion | flops 4033478656 | bytes 10489860 | tf_op jit(solution)/shard_map/dot_general | solution.py:137
  132.4 84.0 %reduce-scatter.5.cloned.1.call-done = bf16[128,2048]{1,0:T(8,128)(2,1)} async-done(((bf16[2048,2048]{1,0:T(8,128)(2,1)}), bf16[128,2048]{1,0:T(8,128)(2,1)}) %reduce-scatter.5.cloned.1.call-update) | async-done | bytes 524304 | tf_op jit(solution)/shard_map/reduce_scatter | solution.py:136
  219.6 10.2 %all-gather.8.cloned.1.call-done = bf16[256,2048]{1,0:T(8,128)(2,1)} async-done(((bf16[128,2048]{1,0:T(8,128)(2,1)}), bf16[256,2048]{1,0:T(8,128)(2,1)}) %all-gather.8.cloned.1.call-update) | async-done | bytes 1048592 | tf_op jit(solution)/shard_map/all_gather | solution.py:157
  236.5 10.2 %collective-permute-done = bf16[128,2048]{1,0:T(8,128)(2,1)S(1)} collective-permute-done((bf16[128,2048]{1,0:T(8,128)(2,1)S(1)}, bf16[128,2048]{1,0:T(8,128)(2,1)S(1)}, u32[]{:S(2)}, u32[]{:S(2)}) %collective-permute-start) | collective-permute-done | bytes 524320 | tf_op jit(solution)/shard_map/ppermute | solution.py:181
  250.1 11.8 %collective-permute-done.2 = bf16[128,2048]{1,0:T(8,128)(2,1)} collective-permute-done((bf16[128,2048]{1,0:T(8,128)(2,1)S(1)}, bf16[128,2048]{1,0:T(8,128)(2,1)}, u32[]{:S(2)}, u32[]{:S(2)}) %collective-permute-start.2) | collective-permute-done | bytes 524320 | tf_op jit(solution)/shard_map/ppermute | solution.py:181
  263.5 102.3 %all-gather.10.cloned.1.call-done = bf16[1,8192,1280]{2,1,0:T(8,128)(2,1)} async-done(((bf16[1,512,1280]{2,1,0:T(8,128)(2,1)}), bf16[1,8192,1280]{2,1,0:T(8,128)(2,1)}) %all-gather.10.cloned.1.call-update) | async-done | bytes 20971536 | tf_op jit(solution)/shard_map/all_gather | solution.py:146
  365.8 9.9 %fusion.35 = bf16[128,1280]{1,0:T(8,128)(2,1)S(1)} fusion(bf16[1,8192,1280]{2,1,0:T(8,128)(2,1)} %all-gather.10.cloned.1.call-done, bf16[128,8192]{1,0:T(8,128)(2,1)S(1)} %constant_dynamic-update-slice_fusion.8, f32[8192]{0:T(1024)S(1)} %bitcast.205, f32[128]{0:T(128)S(1)} %add_rsqrt_fusion.2), kind=kOutput, calls=%fused_computation.41 | convolution fusion | flops 2688712704 | bytes 23429632 | tf_op jit(solution)/shard_map/dot_general | solution.py:192
  376.6 102.2 %all-gather.12.cloned.1.call-done = bf16[1,8192,1024]{2,1,0:T(8,128)(2,1)} async-done(((bf16[1,512,1024]{2,1,0:T(8,128)(2,1)}), bf16[1,8192,1024]{2,1,0:T(8,128)(2,1)}) %all-gather.12.cloned.1.call-update) | async-done | bytes 16777232 | tf_op jit(solution)/shard_map/all_gather | solution.py:147
  478.8 12.7 %fusion.13 = bf16[128,8192]{1,0:T(8,128)(2,1)} fusion(bf16[128,1024]{0,1:T(8,128)(2,1)S(1)} %bitcast.197, bf16[1,8192,1024]{2,1,0:T(8,128)(2,1)} %all-gather.12.cloned.1.call-done), kind=kOutput, calls=%fused_computation.13 | convolution fusion | flops 2148532224 | bytes 19136512 | tf_op jit(solution)/shard_map/dot_general | solution.py:194
  491.6 29.7 %reduce-scatter.7.cloned.1.call-done = bf16[128,2048]{1,0:T(8,128)(2,1)} async-done(((bf16[128,8192]{1,0:T(8,128)(2,1)}), bf16[128,2048]{1,0:T(8,128)(2,1)}) %reduce-scatter.7.cloned.1.call-update) | async-done | bytes 524304 | tf_op jit(solution)/shard_map/reduce_scatter | solution.py:197
  548.2 9.2 %collective-permute-done.6 = bf16[128,2048]{1,0:T(8,128)(2,1)S(1)} collective-permute-done((bf16[128,2048]{1,0:T(8,128)(2,1)S(1)}, bf16[128,2048]{1,0:T(8,128)(2,1)S(1)}, u32[]{:S(2)}, u32[]{:S(2)}) %collective-permute-start.6) | collective-permute-done | bytes 524320 | tf_op jit(solution)/shard_map/ppermute | solution.py:181
  558.0 9.9 %fusion.38 = bf16[128,1280]{1,0:T(8,128)(2,1)S(1)} fusion(bf16[1,8192,1280]{2,1,0:T(8,128)(2,1)} %all-gather.10.cloned.1.call-done, bf16[128,8192]{1,0:T(8,128)(2,1)S(1)} %constant_dynamic-update-slice_fusion.4, f32[128]{0:T(128)S(1)} %add_rsqrt_fusion.1, f32[8192]{0:T(1024)S(1)} %bitcast.206), kind=kOutput, calls=%fused_computation.42 | convolution fusion | flops 2688712704 | bytes 23429632 | tf_op jit(solution)/shard_map/dot_general | solution.py:192
  568.8 12.7 %fusion.16 = bf16[128,8192]{1,0:T(8,128)(2,1)} fusion(bf16[128,1024]{0,1:T(8,128)(2,1)S(1)} %bitcast.199, bf16[1,8192,1024]{2,1,0:T(8,128)(2,1)} %all-gather.12.cloned.1.call-done), kind=kOutput, calls=%fused_computation.14 | convolution fusion | flops 2148532224 | bytes 19136512 | tf_op jit(solution)/shard_map/dot_general | solution.py:194
  581.6 28.7 %reduce-scatter.9.cloned.1.call-done = bf16[128,2048]{1,0:T(8,128)(2,1)} async-done(((bf16[128,8192]{1,0:T(8,128)(2,1)}), bf16[128,2048]{1,0:T(8,128)(2,1)}) %reduce-scatter.9.cloned.1.call-update) | async-done | bytes 524304 | tf_op jit(solution)/shard_map/reduce_scatter | solution.py:197
  618.0 6.9 all-to-all-start
  631.9 7.4 collective-permute-done.10
  645.9 9.9 %fusion.41 = bf16[128,1280]{1,0:T(8,128)(2,1)S(1)} fusion(bf16[1,8192,1280]{2,1,0:T(8,128)(2,1)} %all-gather.10.cloned.1.call-done, bf16[128,8192]{1,0:T(8,128)(2,1)S(1)} %constant_dynamic-update-slice_fusion, f32[128]{0:T(128)S(1)} %add_rsqrt_fusion, f32[8192]{0:T(1024)S(1)} %bitcast.207), kind=kOutput, calls=%fused_computation.43 | convolution fusion | flops 2688712704 | bytes 23429632 | tf_op jit(solution)/shard_map/dot_general | solution.py:192
  656.6 12.8 %fusion.19 = bf16[128,8192]{1,0:T(8,128)(2,1)} fusion(bf16[128,1024]{0,1:T(8,128)(2,1)S(1)} %bitcast.198, bf16[1,8192,1024]{2,1,0:T(8,128)(2,1)} %all-gather.12.cloned.1.call-done), kind=kOutput, calls=%fused_computation.15 | convolution fusion | flops 2148532224 | bytes 19136512 | tf_op jit(solution)/shard_map/dot_general | solution.py:194
  669.5 19.1 %all-to-all-done = bf16[16,64,2048]{2,1,0:T(8,128)(2,1)} async-done(((bf16[16,64,2048]{2,1,0:T(8,128)(2,1)}), bf16[16,64,2048]{2,1,0:T(8,128)(2,1)}, u32[]{:S(2)}, u32[]{:S(2)}) %all-to-all-start) | async-done | bytes 4194336 | tf_op jit(solution)/shard_map/all_to_all | solution.py:212
  688.6 6.5 copy.122
  702.4 46.1 %all-to-all-done.1 = bf16[16,64,2048]{2,0,1:T(8,128)(2,1)} async-done(((bf16[16,64,2048]{2,0,1:T(8,128)(2,1)}), bf16[16,64,2048]{2,0,1:T(8,128)(2,1)}, u32[]{:S(2)}, u32[]{:S(2)}) %all-to-all-start.1) | async-done | bytes 4194336 | tf_op jit(solution)/shard_map/all_to_all | solution.py:211
  (152 shorter events, 101.5 us)
Async XLA Ops:
  7.2 113.8 %all-gather.6.cloned.1.call-start = ((), (), s32[]{:S(2)}) async-start(), calls=%async_computation.6 | async-start | bytes 10649600 | tf_op jit(solution)/shard_map/all_gather | solution.py:117
  32.9 183.5 %reduce-scatter.5.cloned.1.call-start = ((), (), s32[]{:S(2)}) async-start(), calls=%async_computation.7 | async-start | bytes 8912896 | tf_op jit(solution)/shard_map/reduce_scatter | solution.py:136
  131.7 98.1 %all-gather.8.cloned.1.call-start = ((), (), s32[]{:S(2)}) async-start(), calls=%async_computation.8 | async-start | bytes 1572864 | tf_op jit(solution)/shard_map/all_gather | solution.py:157
  218.4 147.4 %all-gather.10.cloned.1.call-start = ((), (), s32[]{:S(2)}) async-start(), calls=%async_computation.9 | async-start | bytes 22282240 | tf_op jit(solution)/shard_map/all_gather | solution.py:146
  219.0 259.8 %all-gather.12.cloned.1.call-start = ((), (), s32[]{:S(2)}) async-start(), calls=%async_computation.10 | async-start | bytes 17825792 | tf_op jit(solution)/shard_map/all_gather | solution.py:147
  219.6 301.7 %reduce-scatter.7.cloned.1.call-start = ((), (), s32[]{:S(2)}) async-start(), calls=%async_computation.11 | async-start | bytes 2621440 | tf_op jit(solution)/shard_map/reduce_scatter | solution.py:197
  231.2 15.5 %collective-permute-start = (bf16[128,2048]{1,0:T(8,128)(2,1)S(1)}, bf16[128,2048]{1,0:T(8,128)(2,1)S(1)}, u32[]{:S(2)}, u32[]{:S(2)}) collective-permute-start(bf16[128,2048]{1,0:T(8,128)(2,1)S(1)} %get-tuple-element.5), channel_id=1, source_target_pairs={{0,1},{1,2},{2,3},{3,0},{4,5},{5,6},{6,7},{7,4},{8,9},{9,10},{10,1... | collective-permute-start | bytes 1572872 | tf_op jit(solution)/shard_map/ppermute | solution.py:181
  234.9 14.1 %collective-permute-start.1 = (bf16[128,2048]{1,0:T(8,128)(2,1)S(1)}, bf16[128,2048]{1,0:T(8,128)(2,1)}, u32[]{:S(2)}, u32[]{:S(2)}) collective-permute-start(bf16[128,2048]{1,0:T(8,128)(2,1)S(1)} %get-tuple-element.5), channel_id=1, source_target_pairs={{0,3},{1,0},{2,1},{3,2},{4,7},{5,4},{6,5},{7,6},{8,11},{9,8},{10,9... | collective-permute-start | bytes 1572872 | tf_op jit(solution)/shard_map/ppermute | solution.py:186
  246.7 15.2 %collective-permute-start.2 = (bf16[128,2048]{1,0:T(8,128)(2,1)S(1)}, bf16[128,2048]{1,0:T(8,128)(2,1)}, u32[]{:S(2)}, u32[]{:S(2)}) collective-permute-start(bf16[128,2048]{1,0:T(8,128)(2,1)S(1)} %collective-permute-done), channel_id=1, source_target_pairs={{0,1},{1,2},{2,3},{3,0},{4,5},{5,6},{6,7},{7,4},{8,9},{9,10},{10,1... | collective-permute-start | bytes 1572872 | tf_op jit(solution)/shard_map/ppermute | solution.py:181
  491.5 118.8 %reduce-scatter.9.cloned.1.call-start = ((), (), s32[]{:S(2)}) async-start(), calls=%async_computation.12 | async-start | bytes 2621440 | tf_op jit(solution)/shard_map/reduce_scatter | solution.py:197
  522.5 3.3 collective-permute-start.3
  527.2 15.5 %collective-permute-start.4 = (bf16[128,2048]{1,0:T(8,128)(2,1)S(1)}, bf16[128,2048]{1,0:T(8,128)(2,1)S(1)}, u32[]{:S(2)}, u32[]{:S(2)}) collective-permute-start(bf16[128,2048]{1,0:T(8,128)(2,1)S(1)} %get-tuple-element.3), channel_id=1, source_target_pairs={{0,1},{1,2},{2,3},{3,0},{4,5},{5,6},{6,7},{7,4},{8,9},{9,10},{10,1... | collective-permute-start | bytes 1572872 | tf_op jit(solution)/shard_map/ppermute | solution.py:181
  527.5 2.9 collective-permute-start.7
  530.4 3.0 collective-permute-start.12
  533.6 14.6 %collective-permute-start.5 = (bf16[128,2048]{1,0:T(8,128)(2,1)S(1)}, bf16[128,2048]{1,0:T(8,128)(2,1)S(1)}, u32[]{:S(2)}, u32[]{:S(2)}) collective-permute-start(bf16[128,2048]{1,0:T(8,128)(2,1)S(1)} %get-tuple-element.3), channel_id=1, source_target_pairs={{0,3},{1,0},{2,1},{3,2},{4,7},{5,4},{6,5},{7,6},{8,11},{9,8},{10,9... | collective-permute-start | bytes 1572872 | tf_op jit(solution)/shard_map/ppermute | solution.py:186
  542.7 14.7 %collective-permute-start.6 = (bf16[128,2048]{1,0:T(8,128)(2,1)S(1)}, bf16[128,2048]{1,0:T(8,128)(2,1)S(1)}, u32[]{:S(2)}, u32[]{:S(2)}) collective-permute-start(bf16[128,2048]{1,0:T(8,128)(2,1)S(1)} %collective-permute-done.4), channel_id=1, source_target_pairs={{0,1},{1,2},{2,3},{3,0},{4,5},{5,6},{6,7},{7,4},{8,9},{9,10},{10,1... | collective-permute-start | bytes 1572872 | tf_op jit(solution)/shard_map/ppermute | solution.py:181
  611.5 3.3 collective-permute-start.8
  614.8 15.5 %collective-permute-start.9 = (bf16[128,2048]{1,0:T(8,128)(2,1)S(1)}, bf16[128,2048]{1,0:T(8,128)(2,1)}, u32[]{:S(2)}, u32[]{:S(2)}) collective-permute-start(bf16[128,2048]{1,0:T(8,128)(2,1)S(1)} %collective-permute-done.8), channel_id=1, source_target_pairs={{0,1},{1,2},{2,3},{3,0},{4,5},{5,6},{6,7},{7,4},{8,9},{9,10},{10,1... | collective-permute-start | bytes 1572872 | tf_op jit(solution)/shard_map/ppermute | solution.py:181
  618.0 70.5 %all-to-all-start = ((bf16[16,64,2048]{2,1,0:T(8,128)(2,1)}), bf16[16,64,2048]{2,1,0:T(8,128)(2,1)}, u32[]{:S(2)}, u32[]{:S(2)}) async-start(bf16[16,64,2048]{2,1,0:T(8,128)(2,1)} %bitcast.188), calls=%async_computation.4 | async-start | bytes 8388608 | tf_op jit(solution)/shard_map/all_to_all | solution.py:212
  624.9 75.2 %reduce-scatter.11.cloned.1.call-start = ((), (), s32[]{:S(2)}) async-start(), calls=%async_computation.13 | async-start | bytes 2621440 | tf_op jit(solution)/shard_map/reduce_scatter | solution.py:197
  625.0 14.3 %collective-permute-start.10 = (bf16[128,2048]{1,0:T(8,128)(2,1)S(1)}, bf16[128,2048]{1,0:T(8,128)(2,1)S(1)}, u32[]{:S(2)}, u32[]{:S(2)}) collective-permute-start(bf16[128,2048]{1,0:T(8,128)(2,1)S(1)} %collective-permute-done.8), channel_id=1, source_target_pairs={{0,3},{1,0},{2,1},{3,2},{4,7},{5,4},{6,5},{7,6},{8,11},{9,8},{10,9... | collective-permute-start | bytes 1572872 | tf_op jit(solution)/shard_map/ppermute | solution.py:186
  630.3 15.0 %collective-permute-start.11 = (bf16[128,2048]{1,0:T(8,128)(2,1)}, bf16[128,2048]{1,0:T(8,128)(2,1)S(1)}, u32[]{:S(2)}, u32[]{:S(2)}) collective-permute-start(bf16[128,2048]{1,0:T(8,128)(2,1)} %collective-permute-done.9), channel_id=1, source_target_pairs={{0,1},{1,2},{2,3},{3,0},{4,5},{5,6},{6,7},{7,4},{8,9},{9,10},{10,1... | collective-permute-start | bytes 1572872 | tf_op jit(solution)/shard_map/ppermute | solution.py:181
  695.0 53.4 %all-to-all-start.1 = ((bf16[16,64,2048]{2,0,1:T(8,128)(2,1)}), bf16[16,64,2048]{2,0,1:T(8,128)(2,1)}, u32[]{:S(2)}, u32[]{:S(2)}) async-start(bf16[16,64,2048]{2,0,1:T(8,128)(2,1)} %copy.122), calls=%async_computation.5 | async-start | bytes 8388608 | tf_op jit(solution)/shard_map/all_to_all | solution.py:211
  700.0 53.1 %all-reduce.3.cloned.1.call-start = ((), (), s32[]{:S(2)}) async-start(), calls=%async_computation.14 | async-start | bytes 2097152 | tf_op jit(solution)/shard_map/psum | solution.py:25
  (14 other events, 411.1 us)
Sparse Core Ops, SparseCore 0:
  33.1 87.8 all-gather.5
  131.8 84.5 reduce-scatter.4
  218.6 11.1 all-gather.7
  231.8 133.9 all-gather.9
  367.8 110.9 all-gather.11
  491.7 29.5 reduce-scatter.6
  581.7 28.5 reduce-scatter.8
  669.6 28.5 reduce-scatter.10
  703.5 24.9 all-reduce.2
